TPU v7x, 32 devices: a whole 2x2x4 slice. The times are simulated.
32 devices in a mesh: sector: 16 (over z, y, x), op: 2 (over core).
Axes of the slice: x: 2, y: 2, z: 4, core: 2. Of those that a mesh axis runs over, the one named last changes fastest.
Arguments:
- psi: bfloat16 [1024, 128, 128], P('sector'), may hold values from -6 to 6
- left_env: bfloat16 [2, 128, 128, 128], P('op', 'sector'), may hold values from -0.5 to 0.5
- right_env: bfloat16 [2, 128, 128, 128], P('op', 'sector'), may hold values from -0.375 to 0.375
- left_dims: int32 [128], replicated, may hold values from 64 to 128
- right_dims: int32 [128], replicated, may hold values from 64 to 128
- block_right: int32 [1024], replicated, may hold values from 0 to 127, as said below
Outputs:
- h_psi: bfloat16 [1024, 128, 128], P('sector', 'op')
Inputs may be any that keep to these rules, and one draw needn't show every extreme that they name: Block d * 64 + j lies in left sector d * 8 + j // 8; its right sector is owned by index block_right // 8 of sector, and block_right % 8 equals j // 8. Of the 64 blocks of each index of sector, exactly 4 have their right sector owned by each index of sector; the 8 blocks of one left sector have distinct right sectors, and every right sector is paired with exactly 8 blocks.
All inputs are finite; a program needn't handle non-finite values.
Results may differ from a plain program's by a relative error of at most 0.0049.
Values may be sent and summed in bfloat16 or wider, within the bound.
A program may use at most 64 MiB of HBM per device.

v0:
```python
import jax
import jax.numpy as jnp
from jax import lax
from jax.sharding import PartitionSpec as P


def combine(partial_sum):
    row_count = partial_sum.shape[1] // lax.axis_size("op")
    whole = lax.psum(partial_sum, "op")
    return lax.dynamic_slice_in_dim(whole, lax.axis_index("op") * row_count, row_count, 1)


def per_device(psi, left_env, right_env, left_dims, right_dims, block_right):
    devices = lax.axis_size("sector")
    sector_index = lax.axis_index("sector")
    blocks = psi.shape[0]
    block_width = psi.shape[1]
    term_count = left_env.shape[0]
    sectors = left_env.shape[1]
    coupled = blocks // sectors
    slot_count = blocks // devices
    counter = jnp.arange(blocks, dtype=jnp.int32)
    mine_right = lax.dynamic_slice_in_dim(block_right, sector_index * blocks, blocks)
    mine_owner = mine_right // sectors
    send_order = jnp.argsort(mine_owner * blocks + counter)
    inverse = jnp.argsort(send_order)
    own_dims = lax.dynamic_slice_in_dim(left_dims, sector_index * sectors, sectors)
    row_limit = jnp.repeat(own_dims, coupled)
    col_limit = right_dims[mine_right]
    position = jnp.arange(block_width, dtype=jnp.int32)
    keep_mask = (position[None, :, None] < row_limit[:, None, None]) & (
        position[None, None, :] < col_limit[:, None, None]
    )
    masked = psi * keep_mask.astype(psi.dtype)
    products = jnp.einsum(
        "ksab,snbc->ksnac",
        left_env,
        masked.reshape(sectors, coupled, block_width, block_width),
        preferred_element_type=jnp.float32,
    )
    products = products.astype(jnp.bfloat16).reshape(term_count, blocks, block_width, block_width)
    owners_all = (block_right // sectors).reshape(devices, blocks)
    foreign = (owners_all != sector_index).astype(jnp.int32)
    incoming = jnp.argsort(foreign * blocks + counter[None, :], axis=1)[:, :slot_count]
    arriving = (
        jnp.take_along_axis(block_right.reshape(devices, blocks), incoming, axis=1).reshape(-1)
        - sector_index * sectors
    )
    outgoing = right_env[:, arriving].reshape(
        term_count, devices, slot_count, block_width, block_width
    )
    received = lax.all_to_all(outgoing, "sector", split_axis=1, concat_axis=1, tiled=True)
    chosen = received.reshape(term_count, blocks, block_width, block_width)[:, inverse]
    partial_sum = jnp.einsum("kjab,kjcb->jac", products, chosen, preferred_element_type=jnp.float32)
    result = combine(partial_sum).astype(jnp.bfloat16)
    row_count = result.shape[1]
    op_index = lax.axis_index("op")
    row_position = op_index * row_count + jnp.arange(row_count, dtype=jnp.int32)
    keep_rows = (row_position[None, :, None] < row_limit[:, None, None]) & (
        position[None, None, :] < col_limit[:, None, None]
    )
    return result * keep_rows.astype(jnp.bfloat16)


def solution(mesh):
    in_specs = (
        P("sector", None, None),
        P("op", "sector", None, None),
        P("op", "sector", None, None),
        P(),
        P(),
        P(),
    )
    out_specs = P("sector", "op", None)
    return jax.shard_map(
        per_device, mesh=mesh, in_specs=in_specs, out_specs=out_specs, check_vma=False
    )
```

profile of v0, /device:TPU:13, one launch (start us, length us, event | category | flops | bytes accessed | tf_op | source)
XLA Modules:
  0.0 86.6 jit_solution(15736413275250530421)
XLA Ops:
  0.0 0.0 copy-start
  0.0 0.8 reshape.167
  0.8 0.7 fusion.4
  1.5 0.1 mul.34
  1.6 0.1 copy.23
  1.7 1.0 %sort.48 = (s32[16,64]{0,1:T(8,128)}, s32[16,64]{0,1:T(8,128)S(1)}) sort(s32[16,64]{0,1:T(8,128)S(1)} %iota_add_fusion, s32[16,64]{0,1:T(8,128)S(1)} %iota.41), dimensions={1}, to_apply=%region_0.1 | sort | flops 10240 | bytes 16384 | tf_op jit(solution)/shard_map/jit(argsort)/sort | solution.py:44
  2.7 0.1 copy.24
  2.8 0.1 reshape.200
  2.9 0.8 gather_fusion.3
  3.7 0.1 reshape.203
  3.8 0.1 copy.25
  3.9 0.1 copy.26
  4.0 0.1 sub.31
  4.1 0.0 copy-done
  4.1 2.2 %gather_fusion.1 = bf16[64,128,128]{2,1,0:T(8,128)(2,1)} fusion(bf16[8,128,128]{2,1,0:T(8,128)(2,1)S(1)} %bitcast.24, s32[1024]{0:T(1024)S(1)} %pad_clamp_fusion.1), kind=kCustom, calls=%fused_computation.1 | custom fusion | bytes 4194560 | tf_op jit(solution)/shard_map/gather | solution.py:49
  6.3 0.0 copy-start.3
  6.3 0.0 copy-start.1
  6.3 6.7 %all-to-all-start = ((bf16[1,16,4,128,128]{4,3,2,0,1:T(8,128)(2,1)}), bf16[1,16,4,128,128]{4,3,2,0,1:T(8,128)(2,1)S(1)}, u32[]{:S(2)}, u32[]{:S(2)}) async-start(bf16[1,16,4,128,128]{4,3,2,0,1:T(8,128)(2,1)} %bitcast.26), calls=%async_computation | async-start | bytes 4194304 | tf_op jit(solution)/shard_map/all_to_all | solution.py:52
  13.0 0.0 copy-done.3
  13.0 0.1 dynamic_slice.9
  13.1 0.1 broadcast_in_dim.10
  13.2 0.1 lt.98
  13.2 0.8 iota_add_fusion.1
  14.0 0.0 copy-done.1
  14.0 0.8 gather_fusion
  14.8 2.0 %sort.49 = (s32[64]{0:T(128)}, s32[64]{0:T(128)S(1)}) sort(s32[64]{0:T(128)S(1)} %get-tuple-element.11, s32[64]{0:T(128)S(1)} %iota.43), dimensions={0}, to_apply=%region_1.2 | sort | flops 384 | bytes 1024 | tf_op jit(solution)/shard_map/jit(argsort)/sort | solution.py:25
  16.9 2.0 %sort.50 = (s32[64]{0:T(128)}, s32[64]{0:T(128)S(1)}) sort(s32[64]{0:T(128)S(1)} %get-tuple-element.9, s32[64]{0:T(128)S(1)} %iota.44), dimensions={0}, to_apply=%region_2.3 | sort | flops 384 | bytes 1024 | tf_op jit(solution)/shard_map/jit(argsort)/sort | solution.py:26
  18.9 0.1 broadcast_compare_fusion
  19.0 0.1 iota_compare_fusion
  19.1 0.0 copy-start.2
  19.1 3.2 %and_select_fusion = bf16[64,128,128]{2,1,0:T(8,128)(2,1)S(1)} fusion(bf16[64,128,128]{2,1,0:T(8,128)(2,1)} %param.6, pred[64,128]{1,0:T(8,128)(4,1)S(1)} %get-tuple-element.14, pred[64,128]{1,0:T(8,128)(4,1)S(1)} %get-tuple-element.13), kind=kLoop, calls=%fused_computation.4 | loop fusion | flops 2097152 | bytes 4210688 | tf_op jit(solution)/shard_map/mul | solution.py:34
  22.3 0.0 copy-done.2
  22.3 2.1 %convolution_convert_fusion = bf16[8,8,128,128]{3,2,1,0:T(8,128)(2,1)} fusion(bf16[8,8,128,128]{3,2,1,0:T(8,128)(2,1)S(1)} %bitcast.27, bf16[1,8,128,128]{3,2,1,0:T(8,128)(2,1)S(1)} %copy-done.2), kind=kOutput, calls=%fused_computation.7 | convolution fusion | flops 269484032 | bytes 4456448 | tf_op jit(solution)/shard_map/ksab,snbc->ksnac/dot_general | solution.py:35
  24.5 36.5 %all-to-all-done = bf16[1,16,4,128,128]{4,3,2,0,1:T(8,128)(2,1)S(1)} async-done(((bf16[1,16,4,128,128]{4,3,2,0,1:T(8,128)(2,1)}), bf16[1,16,4,128,128]{4,3,2,0,1:T(8,128)(2,1)S(1)}, u32[]{:S(2)}, u32[]{:S(2)}) %all-to-all-start) | async-done | bytes 2097184 | tf_op jit(solution)/shard_map/all_to_all | solution.py:52
  61.0 2.2 %gather_fusion.2 = bf16[64,128,128]{2,1,0:T(8,128)(2,1)} fusion(bf16[64,128,128]{2,1,0:T(8,128)(2,1)S(1)} %bitcast.25, s32[1024]{0:T(1024)S(1)} %pad_clamp_fusion), kind=kCustom, calls=%fused_computation.2 | custom fusion | bytes 4194560 | tf_op jit(solution)/shard_map/gather | solution.py:53
  63.1 5.8 %fusion.6 = f32[64,128,128]{2,1,0:T(8,128)} fusion(bf16[64,128,128]{1,2,0:T(8,128)(2,1)} %bitcast.28, bf16[64,128,128]{2,1,0:T(8,128)(2,1)} %gather_fusion.2), kind=kOutput, calls=%fused_computation.38 | convolution fusion | flops 268435456 | bytes 8388608 | tf_op jit(solution)/shard_map/kjab,kjcb->jac/dot_general | solution.py:54
  68.9 16.2 %all-reduce.1 = bf16[64,128,128]{2,1,0:T(8,128)(2,1)S(1)} all-reduce(f32[64,128,128]{2,1,0:T(8,128)} %fusion.6), channel_id=1, replica_groups=mesh['sector'=16,'op'=2] {'op'}, use_global_device_ids=true, to_apply=%region_3.4 | all-reduce | flops 1048576 | bytes 6291456 | tf_op jit(solution)/shard_map/psum | solution.py:9
  85.1 1.5 %and_select_fusion.1 = bf16[64,64,128]{2,1,0:T(8,128)(2,1)} fusion(bf16[64,128,128]{2,1,0:T(8,128)(2,1)S(1)} %all-reduce.1, s32[]{:T(128)S(6)} %select_n.61, pred[64,128]{1,0:T(8,128)(4,1)S(1)} %get-tuple-element.14, pred[64,64]{1,0:T(8,128)(4,1)S(1)} %broadcast_compare_fusion), kind=kLoop, calls=%fused_computation.6 | loop fusion | flops 1048576 | bytes 2109444 | tf_op jit(solution)/shard_map/mul | solution.py:62
  (12 shorter events, 0.1 us)
Async XLA Ops:
  0.0 4.1 %copy-start = (bf16[1,8,128,128]{3,2,1,0:T(8,128)(2,1)S(1)}, bf16[1,8,128,128]{3,2,1,0:T(8,128)(2,1)}, u32[]{:S(2)}) copy-start(bf16[1,8,128,128]{3,2,1,0:T(8,128)(2,1)} %param.8) | copy-start | bytes 786436
  6.3 6.7 %copy-start.3 = (s32[128]{0:T(128)S(1)}, s32[128]{0:T(128)}, u32[]{:S(2)}) copy-start(s32[128]{0:T(128)} %param.9) | copy-start | bytes 1540
  6.3 7.8 %copy-start.1 = (s32[128]{0:T(128)S(1)}, s32[128]{0:T(128)}, u32[]{:S(2)}) copy-start(s32[128]{0:T(128)} %param.10) | copy-start | bytes 1540
  6.3 54.7 %all-to-all-start = ((bf16[1,16,4,128,128]{4,3,2,0,1:T(8,128)(2,1)}), bf16[1,16,4,128,128]{4,3,2,0,1:T(8,128)(2,1)S(1)}, u32[]{:S(2)}, u32[]{:S(2)}) async-start(bf16[1,16,4,128,128]{4,3,2,0,1:T(8,128)(2,1)} %bitcast.26), calls=%async_computation | async-start | bytes 4194304 | tf_op jit(solution)/shard_map/all_to_all | solution.py:52
  19.1 3.2 %copy-start.2 = (bf16[1,8,128,128]{3,2,1,0:T(8,128)(2,1)S(1)}, bf16[1,8,128,128]{3,2,1,0:T(8,128)(2,1)}, u32[]{:S(2)}) copy-start(bf16[1,8,128,128]{3,2,1,0:T(8,128)(2,1)} %param.7) | copy-start | bytes 786436
where the time goes:
time: 86.9 us; the launch traced here: 86.6 us
  waiting for transfers between devices  36.5 us (42%)
  blocking collectives  16.2 us (19%)
  other arithmetic  11.5 us (13%)
  matrix products  7.91 us (9%)
  local copies, waits for them, and re-layouts  7.65 us (9%)
  starting transfers between devices  6.74 us (8%)
    all_to_all x1, waiting for transfers between devices, per_device(): lax.all_to_all(outgoing, 'sector', split_axis=1, concat_axis=1, tiled=True)  36.5 us
    psum x1, blocking collectives, combine(): whole = lax.psum(partial_sum, 'op')  16.2 us
    all_to_all x1, starting transfers between devices, per_device(): lax.all_to_all(outgoing, 'sector', split_axis=1, concat_axis=1, tiled=True)  6.74 us
    dot_general x1, matrix products, per_device(): jnp.einsum('kjab,kjcb->jac', products, chosen, preferred_element_type=jnp...  5.76 us
    mul x1, other arithmetic, per_device(): masked = psi * keep_mask.astype(psi.dtype)  3.23 us
    gather x1, local copies, waits for them, and re-layouts, per_device(): right_env[:, arriving]  2.17 us
    gather x1, local copies, waits for them, and re-layouts, per_device(): received.reshape(term_count, blocks, block_width, block_width)[:, inverse]  2.16 us
    dot_general x1, matrix products, per_device(): jnp.einsum('ksab,snbc->ksnac', left_env, masked.reshape(sectors, coupled,...  2.15 us
  transfers between devices with their start and end apart: 1, of which 1 were waited for; matrix products, arithmetic and copies ran while one was open for 13% of the time, Pallas kernels for 0%

commit v1 on v0

--- a/solution.py
+++ b/solution.py
@@ -49,7 +49,12 @@
     outgoing = right_env[:, arriving].reshape(
         term_count, devices, slot_count, block_width, block_width
     )
-    received = lax.all_to_all(outgoing, "sector", split_axis=1, concat_axis=1, tiled=True)
+    received = jnp.concatenate(
+        lax.all_to_all(
+            jnp.stack(jnp.split(outgoing, lax.axis_size("sector"), axis=1)), "sector", 0, 0
+        ),
+        axis=1,
+    )
     chosen = received.reshape(term_count, blocks, block_width, block_width)[:, inverse]
     partial_sum = jnp.einsum("kjab,kjcb->jac", products, chosen, preferred_element_type=jnp.float32)
     result = combine(partial_sum).astype(jnp.bfloat16)

time: 86.9 us -> 97 us (1.12)
  local copies, waits for them, and re-layouts: 7.65 us -> 17 us
    unnamed x8 -> x23, local copies, waits for them, and re-layouts: 0.02 us -> 9.88 us
    gather x1, local copies, waits for them, and re-layouts: 2.17 us -> 0.95 us  [per_device(): right_env[:, arriving]]
  transfers between devices with their start and end apart: 1 -> 1, of which waited for: 1 -> 1; matrix products, arithmetic and copies ran while one was open for 13% -> 11% of each run, Pallas kernels for 0% -> 0%
where the time goes in v1:
time: 97 us; the launch traced here: 96.7 us
  waiting for transfers between devices  37.2 us (38%)
  local copies, waits for them, and re-layouts  17 us (18%)
  blocking collectives  16.2 us (17%)
  other arithmetic  11.6 us (12%)
  matrix products  7.91 us (8%)
  starting transfers between devices  6.74 us (7%)
    all_to_all x1, waiting for transfers between devices, per_device(): lax.all_to_all(jnp.stack(jnp.split(outgoing, lax.axis_size('sector'), axi...  37.2 us
    psum x1, blocking collectives, combine(): whole = lax.psum(partial_sum, 'op')  16.2 us
    unnamed x23, local copies, waits for them, and re-layouts  9.88 us
    all_to_all x1, starting transfers between devices, per_device(): lax.all_to_all(jnp.stack(jnp.split(outgoing, lax.axis_size('sector'), axi...  6.74 us
    dot_general x1, matrix products, per_device(): jnp.einsum('kjab,kjcb->jac', products, chosen, preferred_element_type=jnp...  5.76 us
    mul x1, other arithmetic, per_device(): masked = psi * keep_mask.astype(psi.dtype)  3.23 us
    gather x1, local copies, waits for them, and re-layouts, per_device(): received.reshape(term_count, blocks, block_width, block_width)[:, inverse]  2.16 us
    dot_general x1, matrix products, per_device(): jnp.einsum('ksab,snbc->ksnac', left_env, masked.reshape(sectors, coupled,...  2.15 us
  transfers between devices with their start and end apart: 1, of which 1 were waited for; matrix products, arithmetic and copies ran while one was open for 11% of the time, Pallas kernels for 0%

profile of v1, /device:TPU:13, one launch (start us, length us, event | category | flops | bytes accessed | tf_op | source)
XLA Modules:
  0.0 96.7 jit_solution(10176076833489912751)
XLA Ops:
  0.0 0.0 copy-start
  0.0 0.8 reshape.164
  0.8 0.7 fusion.20
  1.5 0.8 iota_add_fusion.1
  2.3 0.1 mul.34
  2.3 0.1 copy.17
  2.4 1.0 %sort.48 = (s32[16,64]{0,1:T(8,128)}, s32[16,64]{0,1:T(8,128)S(1)}) sort(s32[16,64]{0,1:T(8,128)S(1)} %iota_add_fusion, s32[16,64]{0,1:T(8,128)S(1)} %iota.41), dimensions={1}, to_apply=%region_0.1 | sort | flops 10240 | bytes 16384 | tf_op jit(solution)/shard_map/jit(argsort)/sort | solution.py:44
  3.5 0.1 copy.18
  3.6 0.1 reshape.196
  3.7 0.8 gather_fusion.3
  4.5 0.1 reshape.199
  4.5 0.1 copy.19
  4.6 0.1 copy.20
  4.7 0.1 sub.31
  4.9 0.0 copy-done
  4.9 1.0 gather_fusion.1
  5.8 0.6 fusion.16
  6.5 0.7 fusion.15
  7.1 0.7 fusion.14
  7.8 0.7 fusion.13
  8.5 0.7 fusion.12
  9.1 0.6 fusion.11
  9.8 0.7 fusion.10
  10.4 0.7 fusion.9
  11.1 0.7 fusion.8
  11.8 0.7 fusion.7
  12.4 0.7 fusion.6
  13.1 0.7 fusion.5
  13.7 0.7 fusion.4
  14.4 0.7 fusion.3
  15.0 0.6 fusion.2
  15.7 0.7 fusion.1
  16.4 0.0 copy-start.3
  16.4 0.0 copy-start.1
  16.4 6.7 %all-to-all-start = ((bf16[16,1,1,4,128,128]{5,4,3,2,1,0:T(8,128)(2,1)}), bf16[16,1,1,4,128,128]{5,4,3,2,1,0:T(8,128)(2,1)S(1)}, u32[]{:S(2)}, u32[]{:S(2)}) async-start(bf16[16,1,1,4,128,128]{5,4,3,2,1,0:T(8,128)(2,1)} %fusion.1), calls=%async_computation | async-start | bytes 4194304 | tf_op jit(solution)/shard_map/all_to_all | solution.py:53
  23.1 0.0 copy-done.3
  23.1 0.1 dynamic_slice.9
  23.2 0.1 broadcast_in_dim.10
  23.3 0.1 lt.98
  23.3 2.0 %sort.49 = (s32[64]{0:T(128)}, s32[64]{0:T(128)S(1)}) sort(s32[64]{0:T(128)S(1)} %get-tuple-element.11, s32[64]{0:T(128)S(1)} %iota.43), dimensions={0}, to_apply=%region_1.2 | sort | flops 384 | bytes 1024 | tf_op jit(solution)/shard_map/jit(argsort)/sort | solution.py:25
  25.4 2.0 %sort.50 = (s32[64]{0:T(128)}, s32[64]{0:T(128)S(1)}) sort(s32[64]{0:T(128)S(1)} %get-tuple-element.9, s32[64]{0:T(128)S(1)} %iota.44), dimensions={0}, to_apply=%region_2.3 | sort | flops 384 | bytes 1024 | tf_op jit(solution)/shard_map/jit(argsort)/sort | solution.py:26
  27.4 0.0 copy-done.1
  27.4 0.8 gather_fusion
  28.2 0.1 iota_compare_fusion.1
  28.3 0.1 iota_compare_fusion
  28.4 0.1 broadcast_compare_fusion
  28.5 0.0 copy-start.2
  28.5 3.2 %and_select_fusion = bf16[64,128,128]{2,1,0:T(8,128)(2,1)S(1)} fusion(bf16[64,128,128]{2,1,0:T(8,128)(2,1)} %param.6, pred[64,128]{1,0:T(8,128)(4,1)S(1)} %iota_compare_fusion.1, pred[64,128]{1,0:T(8,128)(4,1)S(1)} %iota_compare_fusion), kind=kLoop, calls=%fused_computation.4 | loop fusion | flops 2097152 | bytes 4210688 | tf_op jit(solution)/shard_map/mul | solution.py:34
  31.7 0.0 copy-done.2
  31.7 2.1 %convolution_convert_fusion = bf16[8,8,128,128]{3,2,1,0:T(8,128)(2,1)} fusion(bf16[8,8,128,128]{3,2,1,0:T(8,128)(2,1)S(1)} %bitcast.106, bf16[1,8,128,128]{3,2,1,0:T(8,128)(2,1)S(1)} %copy-done.2), kind=kOutput, calls=%fused_computation.7 | convolution fusion | flops 269484032 | bytes 4456448 | tf_op jit(solution)/shard_map/ksab,snbc->ksnac/dot_general | solution.py:35
  33.9 37.2 %all-to-all-done = bf16[16,1,1,4,128,128]{5,4,3,2,1,0:T(8,128)(2,1)S(1)} async-done(((bf16[16,1,1,4,128,128]{5,4,3,2,1,0:T(8,128)(2,1)}), bf16[16,1,1,4,128,128]{5,4,3,2,1,0:T(8,128)(2,1)S(1)}, u32[]{:S(2)}, u32[]{:S(2)}) %all-to-all-start) | async-done | bytes 2097184 | tf_op jit(solution)/shard_map/all_to_all | solution.py:53
  71.1 2.2 %gather_fusion.2 = bf16[64,128,128]{2,1,0:T(8,128)(2,1)} fusion(bf16[64,128,128]{2,1,0:T(8,128)(2,1)S(1)} %bitcast.105, s32[1024]{0:T(1024)S(1)} %pad_clamp_fusion), kind=kCustom, calls=%fused_computation.2 | custom fusion | bytes 4194560 | tf_op jit(solution)/shard_map/gather | solution.py:58
  73.2 5.8 %fusion.22 = f32[64,128,128]{2,1,0:T(8,128)} fusion(bf16[64,128,128]{1,2,0:T(8,128)(2,1)} %bitcast.107, bf16[64,128,128]{2,1,0:T(8,128)(2,1)} %gather_fusion.2), kind=kOutput, calls=%fused_computation.70 | convolution fusion | flops 268435456 | bytes 8388608 | tf_op jit(solution)/shard_map/kjab,kjcb->jac/dot_general | solution.py:59
  79.0 16.2 %all-reduce.1 = bf16[64,128,128]{2,1,0:T(8,128)(2,1)S(1)} all-reduce(f32[64,128,128]{2,1,0:T(8,128)} %fusion.22), channel_id=1, replica_groups=mesh['sector'=16,'op'=2] {'op'}, use_global_device_ids=true, to_apply=%region_3.4 | all-reduce | flops 1048576 | bytes 6291456 | tf_op jit(solution)/shard_map/psum | solution.py:9
  95.2 1.5 %and_select_fusion.1 = bf16[64,64,128]{2,1,0:T(8,128)(2,1)} fusion(bf16[64,128,128]{2,1,0:T(8,128)(2,1)S(1)} %all-reduce.1, s32[]{:T(128)S(6)} %select_n.61, pred[64,128]{1,0:T(8,128)(4,1)S(1)} %iota_compare_fusion.1, pred[64,64]{1,0:T(8,128)(4,1)S(1)} %broadcast_compare_fusion), kind=kLoop, calls=%fused_computation.6 | loop fusion | flops 1048576 | bytes 2109444 | tf_op jit(solution)/shard_map/mul | solution.py:67
  (11 shorter events, 0.1 us)
Async XLA Ops:
  0.0 4.9 %copy-start = (bf16[1,8,128,128]{3,2,1,0:T(8,128)(2,1)S(1)}, bf16[1,8,128,128]{3,2,1,0:T(8,128)(2,1)}, u32[]{:S(2)}) copy-start(bf16[1,8,128,128]{3,2,1,0:T(8,128)(2,1)} %param.8) | copy-start | bytes 786436
  16.4 6.7 %copy-start.3 = (s32[128]{0:T(128)S(1)}, s32[128]{0:T(128)}, u32[]{:S(2)}) copy-start(s32[128]{0:T(128)} %param.9) | copy-start | bytes 1540
  16.4 11.1 %copy-start.1 = (s32[128]{0:T(128)S(1)}, s32[128]{0:T(128)}, u32[]{:S(2)}) copy-start(s32[128]{0:T(128)} %param.10) | copy-start | bytes 1540
  16.4 54.7 %all-to-all-start = ((bf16[16,1,1,4,128,128]{5,4,3,2,1,0:T(8,128)(2,1)}), bf16[16,1,1,4,128,128]{5,4,3,2,1,0:T(8,128)(2,1)S(1)}, u32[]{:S(2)}, u32[]{:S(2)}) async-start(bf16[16,1,1,4,128,128]{5,4,3,2,1,0:T(8,128)(2,1)} %fusion.1), calls=%async_computation | async-start | bytes 4194304 | tf_op jit(solution)/shard_map/all_to_all | solution.py:53
  28.5 3.2 %copy-start.2 = (bf16[1,8,128,128]{3,2,1,0:T(8,128)(2,1)S(1)}, bf16[1,8,128,128]{3,2,1,0:T(8,128)(2,1)}, u32[]{:S(2)}) copy-start(bf16[1,8,128,128]{3,2,1,0:T(8,128)(2,1)} %param.7) | copy-start | bytes 786436
